TPU v7x, 512 devices: a whole 4x8x8 slice. The times are simulated.
512 devices in a mesh: ops: 32 (over x, z), sec: 16 (over y, core).
Axes of the slice: x: 4, y: 8, z: 8, core: 2. Of those that a mesh axis runs over, the one named last changes fastest.
Arguments:
- sector_states: int32 [16], P('sec'), may hold values from 85 to 256, as said below
- psi_guess: bfloat16 [16, 256, 256], P('sec'), may hold values from -6 to 6
- precond_diag: bfloat16 [16, 256, 256], P('sec'), may hold values from -12 to 12
- left_ops: float32 [64, 16, 256, 256], P('ops', 'sec'), may hold values from -0.375 to 0.375
- right_ops: float32 [64, 16, 256, 256], P('ops', 'sec'), may hold values from -0.375 to 0.375
- couple: int32 [64, 16], P('ops', 'sec'), may hold values from -1 to 15, as said below
- new_sector: int32 [16], P('sec'), may hold values from 0 to 15, as said below
Outputs:
- wavefunction: float32 [16, 256, 256], P('sec')
- rotated_ops: float32 [64, 16, 256, 256], P('ops', 'sec')
Inputs may be any that keep to these rules, and one draw needn't show every extreme that they name: `sector_states`: at least one sector has 256 states. couple[p, s] is s - 1, s or s + 1, or -1 where that lies outside the sectors. `new_sector`: each aligned pair of sectors 2k, 2k + 1 either keeps its labels or swaps them; the pair with 2k = 8 always swaps.
All inputs are finite; a program needn't handle non-finite values.
Results may differ from a plain program's by a relative error of at most 0.0003.
Values sent between devices are 32-bit elements; how exact they have to be, the bound alone decides.
A program may use at most 64 MiB of HBM per device.

v0:
```python
import jax
import jax.numpy as jnp
from jax import lax
from jax.sharding import PartitionSpec as P

UPDATES = 2


HIGH = lax.Precision.HIGHEST


def extended(cells, sides, width):
    for axis, dim in sides:
        count = lax.axis_size(axis)
        ends = count - 1
        head = lax.slice_in_dim(cells, 0, width, axis=dim)
        tail = lax.slice_in_dim(cells, cells.shape[dim] - width, cells.shape[dim], axis=dim)
        cells = jnp.concatenate(
            [
                lax.ppermute(tail, axis, [(i, (i + 1) % count) for i in range(ends)]),
                cells,
                lax.ppermute(head, axis, [((i + 1) % count, i) for i in range(ends)]),
            ],
            axis=dim,
        )
    return cells


def cut_along(x, dim, devices):
    before, after = (x.shape[:dim], x.shape[dim + 1 :])
    return jnp.moveaxis(x.reshape(*before, devices, -1, *after), dim, 0)


def summed_on_arrival(x, axis, dim):
    devices = lax.axis_size(axis)
    parts = lax.all_to_all(cut_along(x, dim, devices), axis, 0, 0, tiled=True)
    return jnp.sum(parts, axis=0)


def padded_to(lines, devices):
    spare = -lines.shape[0] % devices
    if not spare:
        return lines
    return jnp.concatenate([lines, jnp.zeros((spare, *lines.shape[1:]), lines.dtype)])


def joined_along(parts, dim):
    parts = jnp.moveaxis(parts, 0, dim)
    dims = parts.shape
    return parts.reshape(*dims[:dim], dims[dim] * dims[dim + 1], *dims[dim + 2 :])


def sent_to_all(x, axis):
    copies = jnp.broadcast_to(x, (lax.axis_size(axis), *x.shape))
    return lax.all_to_all(copies, axis, split_axis=0, concat_axis=0, tiled=True)


def collect(x, axis, dim):
    return joined_along(sent_to_all(x, axis), dim)


def total_of(x, axes):
    lines = x.reshape(-1, x.shape[-1])
    own = summed_on_arrival(padded_to(lines, lax.axis_size(axes)), axes, 0)
    whole = collect(own, axes, 0)
    return whole[: len(lines)].reshape(x.shape)


def over_copies(x, axis):
    everything = sent_to_all(x, axis)
    return jnp.sum(everything, axis=0)


def swapped(block, axis, bit):
    count = lax.axis_size(axis)
    route = []
    for low in range(count):
        high = low | 1 << bit
        if high != low and high < count:
            route += [(low, high), (high, low)]
    return lax.ppermute(block, axis, route)


def local(sector_states, psi_guess, precond_diag, left_ops, right_ops, couple, new_sector):
    block = psi_guess.shape[1]
    here = lax.axis_index("sec")
    sectors = lax.axis_size("sec")
    index = jnp.arange(block, dtype=jnp.int32)
    size_here = sector_states[0]
    live = ((index[:, None] < size_here) & (index[None, :] < size_here)).astype(jnp.float32)[None]
    source = couple[:, 0]
    offset = source - here + 1
    picks = jnp.stack(
        [((offset == k) & (source >= 0)).astype(jnp.float32) for k in range(3)], axis=1
    )
    lefts = left_ops[:, 0]
    rights = right_ops[:, 0]
    diag_rows = precond_diag.astype(jnp.float32)

    def widen(full):
        return extended(full, (("sec", 0),), 1)

    def product(wide):
        chosen = jnp.einsum("pk,kij->pij", picks, wide, precision=HIGH)
        mixed = jnp.einsum("pij,pjk->pik", lefts, chosen, precision=HIGH)
        terms = jnp.einsum("pik,plk->il", mixed, rights, precision=HIGH)[None]
        summed = total_of(terms, "ops")
        return summed * live

    def totals(values):
        return jax.tree.map(lambda part: over_copies(part, "sec"), values)

    start = psi_guess.astype(jnp.float32) * live
    start_wide = widen(start)
    h_start = product(start_wide)
    squares, energy = totals((jnp.sum(start * start), jnp.sum(start * h_start)))
    factor = lax.rsqrt(squares + 1e-06)
    vecx = start * factor
    hvec = h_start * factor
    wide_x = start_wide * factor
    theta = energy * factor * factor
    for update in range(UPDATES):
        corr = live * (hvec - theta * vecx) / (jnp.abs(diag_rows - theta) + 1.0)
        correlation = totals((jnp.sum(vecx * corr),))[0]
        corr = corr - correlation * vecx
        length = totals((jnp.sum(corr * corr),))[0]
        corr = corr * lax.rsqrt(length + 1e-06)
        wide_c = widen(corr)
        hcorr = product(wide_c)
        cross_a, cross_b, last = totals(
            (jnp.sum(vecx * hcorr), jnp.sum(corr * hvec), jnp.sum(corr * hcorr))
        )
        middle = 0.5 * (cross_a + cross_b)
        angle = 0.5 * jnp.arctan2(-2.0 * middle, last - theta)
        cosine = jnp.cos(angle)
        sine = jnp.sin(angle)
        vecx = cosine * vecx + sine * corr
        hvec = cosine * hvec + sine * hcorr
        wide_x = cosine * wide_x + sine * wide_c
        theta = 0.5 * (theta + last) - 0.5 * jnp.sqrt((last - theta) ** 2 + 4.0 * middle * middle)
    scaled = wide_x * jnp.sqrt(jnp.float32(sectors * block * block))
    wavefunction = scaled[1:2]
    chosen = jnp.einsum("pk,kij->pij", picks, scaled, precision=HIGH)
    inner = jnp.einsum("pjk,pkl->pjl", lefts, chosen, precision=HIGH)
    turned = jnp.einsum("ji,pjl->pil", scaled[1], inner, precision=HIGH) / jnp.sqrt(
        jnp.float32(block)
    )
    partner = swapped(turned, "sec", 0)
    keep = new_sector[0] == here
    rotated_ops = jnp.where(keep, turned, partner)[:, None]
    return (wavefunction, rotated_ops)


def solution(mesh):
    in_specs = (
        P("sec"),
        P("sec", None, None),
        P("sec", None, None),
        P("ops", "sec", None, None),
        P("ops", "sec", None, None),
        P("ops", "sec"),
        P("sec"),
    )
    out_specs = (P("sec", None, None), P("ops", "sec", None, None))
    return jax.shard_map(local, mesh=mesh, in_specs=in_specs, out_specs=out_specs, check_vma=False)
```

profile of v0, /device:TPU:1, one launch (start us, length us, event | category | flops | bytes accessed | tf_op | source)
XLA Modules:
  0.0 336.1 jit_solution(10058200515585977026)
XLA Ops:
  3.1 8.7 %collective-permute-start.1 = (f32[1,256,256]{2,0,1:T(1,128)S(1)}, f32[1,256,256]{2,0,1:T(1,128)S(1)}, u32[]{:S(2)}, u32[]{:S(2)}) collective-permute-start(f32[1,256,256]{2,0,1:T(1,128)S(1)} %and_select_fusion.5), channel_id=1, source_target_pairs={{1,0},{2,1},{3,2},{4,3},{5,4},{6,5},{7,6},{8,7},{9,8},{10,9},{11,1... | collective-permute-start | bytes 786440 | tf_op jit(solution)/shard_map/ppermute | solution.py:22
  20.5 19.2 %all_to_all.102 = f32[32,8,256]{2,1,0:T(8,128)S(1)} all-to-all(f32[32,8,256]{2,1,0:T(8,128)S(1)} %convolution_bitcast_fusion.6), channel_id=1, replica_groups=mesh['ops'=32,'sec'=16] {'ops'}, dimensions={0} | all-to-all | bytes 524288 | tf_op jit(solution)/shard_map/all_to_all | solution.py:36
  39.8 14.5 %all_to_all.103 = f32[32,8,256]{2,1,0:T(8,128)S(1)} all-to-all(f32[32,8,256]{2,1,0:T(8,128)S(1)} %broadcast_in_dim.52), channel_id=1, replica_groups=mesh['ops'=32,'sec'=16] {'ops'}, dimensions={0} | all-to-all | bytes 524288 | tf_op jit(solution)/shard_map/all_to_all | solution.py:55
  59.0 17.7 %all_to_all.104 = f32[16,1,1]{2,1,0:T(1,128)S(1)} all-to-all(f32[16,1,1]{2,1,0:T(1,128)S(1)} %broadcast_in_dim.51), channel_id=1, replica_groups=mesh['ops'=32,'sec'=16] {'sec'}, dimensions={0} | all-to-all | bytes 128 | tf_op jit(solution)/shard_map/all_to_all | solution.py:55
  77.9 3.9 %all-to-all-start.3 = ((f32[16,1,1]{2,1,0:T(1,128)}), f32[16,1,1]{2,1,0:T(1,128)S(1)}, u32[]{:S(2)}, u32[]{:S(2)}) async-start(f32[16,1,1]{2,1,0:T(1,128)} %broadcast_in_dim.53), calls=%async_computation.3 | async-start | bytes 16384 | tf_op jit(solution)/shard_map/all_to_all | solution.py:55
  83.2 5.7 %all-to-all-done.3 = f32[16,1,1]{2,1,0:T(1,128)S(1)} async-done(((f32[16,1,1]{2,1,0:T(1,128)}), f32[16,1,1]{2,1,0:T(1,128)S(1)}, u32[]{:S(2)}, u32[]{:S(2)}) %all-to-all-start.3) | async-done | bytes 96 | tf_op jit(solution)/shard_map/all_to_all | solution.py:55
  93.9 10.1 %all_to_all.105 = f32[16,1,1]{2,1,0:T(1,128)S(1)} all-to-all(f32[16,1,1]{2,1,0:T(1,128)S(1)} %broadcast_in_dim.54), channel_id=1, replica_groups=mesh['ops'=32,'sec'=16] {'sec'}, dimensions={0} | all-to-all | bytes 128 | tf_op jit(solution)/shard_map/all_to_all | solution.py:55
  108.7 10.1 %all_to_all.106 = f32[16,1,1]{2,1,0:T(1,128)S(1)} all-to-all(f32[16,1,1]{2,1,0:T(1,128)S(1)} %broadcast_in_dim.55), channel_id=1, replica_groups=mesh['ops'=32,'sec'=16] {'sec'}, dimensions={0} | all-to-all | bytes 128 | tf_op jit(solution)/shard_map/all_to_all | solution.py:55
  134.7 14.8 %all_to_all.107 = f32[32,8,256]{2,1,0:T(8,128)S(1)} all-to-all(f32[32,8,256]{2,1,0:T(8,128)S(1)} %convolution_bitcast_fusion.5), channel_id=1, replica_groups=mesh['ops'=32,'sec'=16] {'ops'}, dimensions={0} | all-to-all | bytes 524288 | tf_op jit(solution)/shard_map/all_to_all | solution.py:36
  149.5 15.2 %all_to_all.108 = f32[32,8,256]{2,1,0:T(8,128)S(1)} all-to-all(f32[32,8,256]{2,1,0:T(8,128)S(1)} %broadcast_in_dim.56), channel_id=1, replica_groups=mesh['ops'=32,'sec'=16] {'ops'}, dimensions={0} | all-to-all | bytes 524288 | tf_op jit(solution)/shard_map/all_to_all | solution.py:55
  169.0 13.9 %all_to_all.109 = f32[16,1,1]{2,1,0:T(1,128)S(1)} all-to-all(f32[16,1,1]{2,1,0:T(1,128)S(1)} %broadcast_in_dim.58), channel_id=1, replica_groups=mesh['ops'=32,'sec'=16] {'sec'}, dimensions={0} | all-to-all | bytes 128 | tf_op jit(solution)/shard_map/all_to_all | solution.py:55
  184.1 3.9 %all-to-all-start.8 = ((f32[16,1,1]{2,1,0:T(1,128)}), f32[16,1,1]{2,1,0:T(1,128)S(1)}, u32[]{:S(2)}, u32[]{:S(2)}) async-start(f32[16,1,1]{2,1,0:T(1,128)} %broadcast_in_dim.57), calls=%async_computation.8 | async-start | bytes 16384 | tf_op jit(solution)/shard_map/all_to_all | solution.py:55
  188.6 6.4 %all-to-all-done.8 = f32[16,1,1]{2,1,0:T(1,128)S(1)} async-done(((f32[16,1,1]{2,1,0:T(1,128)}), f32[16,1,1]{2,1,0:T(1,128)S(1)}, u32[]{:S(2)}, u32[]{:S(2)}) %all-to-all-start.8) | async-done | bytes 96 | tf_op jit(solution)/shard_map/all_to_all | solution.py:55
  196.3 3.9 %all-to-all-start.10 = ((f32[16,1,1]{2,1,0:T(1,128)}), f32[16,1,1]{2,1,0:T(1,128)S(1)}, u32[]{:S(2)}, u32[]{:S(2)}) async-start(f32[16,1,1]{2,1,0:T(1,128)} %broadcast_in_dim.59), calls=%async_computation.10 | async-start | bytes 16384 | tf_op jit(solution)/shard_map/all_to_all | solution.py:55
  202.2 5.0 %all-to-all-done.10 = f32[16,1,1]{2,1,0:T(1,128)S(1)} async-done(((f32[16,1,1]{2,1,0:T(1,128)}), f32[16,1,1]{2,1,0:T(1,128)S(1)}, u32[]{:S(2)}, u32[]{:S(2)}) %all-to-all-start.10) | async-done | bytes 96 | tf_op jit(solution)/shard_map/all_to_all | solution.py:55
  213.5 10.1 %all_to_all.110 = f32[16,1,1]{2,1,0:T(1,128)S(1)} all-to-all(f32[16,1,1]{2,1,0:T(1,128)S(1)} %broadcast_in_dim.60), channel_id=1, replica_groups=mesh['ops'=32,'sec'=16] {'sec'}, dimensions={0} | all-to-all | bytes 128 | tf_op jit(solution)/shard_map/all_to_all | solution.py:55
  226.8 10.1 %all_to_all.111 = f32[16,1,1]{2,1,0:T(1,128)S(1)} all-to-all(f32[16,1,1]{2,1,0:T(1,128)S(1)} %broadcast_in_dim.61), channel_id=1, replica_groups=mesh['ops'=32,'sec'=16] {'sec'}, dimensions={0} | all-to-all | bytes 128 | tf_op jit(solution)/shard_map/all_to_all | solution.py:55
  251.0 15.1 %all_to_all.112 = f32[32,8,256]{2,1,0:T(8,128)S(1)} all-to-all(f32[32,8,256]{2,1,0:T(8,128)S(1)} %convolution_bitcast_fusion.4), channel_id=1, replica_groups=mesh['ops'=32,'sec'=16] {'ops'}, dimensions={0} | all-to-all | bytes 524288 | tf_op jit(solution)/shard_map/all_to_all | solution.py:36
  266.1 15.0 %all_to_all.113 = f32[32,8,256]{2,1,0:T(8,128)S(1)} all-to-all(f32[32,8,256]{2,1,0:T(8,128)S(1)} %broadcast_in_dim.62), channel_id=1, replica_groups=mesh['ops'=32,'sec'=16] {'ops'}, dimensions={0} | all-to-all | bytes 524288 | tf_op jit(solution)/shard_map/all_to_all | solution.py:55
  284.3 14.1 %all_to_all.114 = f32[16,1,1]{2,1,0:T(1,128)S(1)} all-to-all(f32[16,1,1]{2,1,0:T(1,128)S(1)} %broadcast_in_dim.64), channel_id=1, replica_groups=mesh['ops'=32,'sec'=16] {'sec'}, dimensions={0} | all-to-all | bytes 128 | tf_op jit(solution)/shard_map/all_to_all | solution.py:55
  299.7 3.9 %all-to-all-start.15 = ((f32[16,1,1]{2,1,0:T(1,128)}), f32[16,1,1]{2,1,0:T(1,128)S(1)}, u32[]{:S(2)}, u32[]{:S(2)}) async-start(f32[16,1,1]{2,1,0:T(1,128)} %broadcast_in_dim.63), calls=%async_computation.15 | async-start | bytes 16384 | tf_op jit(solution)/shard_map/all_to_all | solution.py:55
  304.3 6.4 %all-to-all-done.15 = f32[16,1,1]{2,1,0:T(1,128)S(1)} async-done(((f32[16,1,1]{2,1,0:T(1,128)}), f32[16,1,1]{2,1,0:T(1,128)S(1)}, u32[]{:S(2)}, u32[]{:S(2)}) %all-to-all-start.15) | async-done | bytes 96 | tf_op jit(solution)/shard_map/all_to_all | solution.py:55
  311.9 4.0 %all-to-all-start.17 = ((f32[16,1,1]{2,1,0:T(1,128)}), f32[16,1,1]{2,1,0:T(1,128)S(1)}, u32[]{:S(2)}, u32[]{:S(2)}) async-start(f32[16,1,1]{2,1,0:T(1,128)} %broadcast_in_dim.65), calls=%async_computation.17 | async-start | bytes 16384 | tf_op jit(solution)/shard_map/all_to_all | solution.py:55
  317.6 5.3 %all-to-all-done.17 = f32[16,1,1]{2,1,0:T(1,128)S(1)} async-done(((f32[16,1,1]{2,1,0:T(1,128)}), f32[16,1,1]{2,1,0:T(1,128)S(1)}, u32[]{:S(2)}, u32[]{:S(2)}) %all-to-all-start.17) | async-done | bytes 96 | tf_op jit(solution)/shard_map/all_to_all | solution.py:55
  (105 shorter events, 88.6 us)
Async XLA Ops:
  0.6 18.2 %copy-start = (f32[2,1,256,256]{3,2,1,0:T(8,128)S(1)}, f32[2,1,256,256]{3,2,1,0:T(8,128)}, u32[]{:S(2)}) copy-start(f32[2,1,256,256]{3,2,1,0:T(8,128)} %param.10) | copy-start | bytes 1572868
  3.1 11.6 %collective-permute-start.1 = (f32[1,256,256]{2,0,1:T(1,128)S(1)}, f32[1,256,256]{2,0,1:T(1,128)S(1)}, u32[]{:S(2)}, u32[]{:S(2)}) collective-permute-start(f32[1,256,256]{2,0,1:T(1,128)S(1)} %and_select_fusion.5), channel_id=1, source_target_pairs={{1,0},{2,1},{3,2},{4,3},{5,4},{6,5},{7,6},{8,7},{9,8},{10,9},{11,1... | collective-permute-start | bytes 786440 | tf_op jit(solution)/shard_map/ppermute | solution.py:22
  11.9 5.2 %collective-permute-start = (f32[1,256,256]{2,0,1:T(1,128)S(1)}, f32[1,256,256]{2,0,1:T(1,128)S(1)}, u32[]{:S(2)}, u32[]{:S(2)}) collective-permute-start(f32[1,256,256]{2,0,1:T(1,128)S(1)} %and_select_fusion.5), channel_id=1, source_target_pairs={{0,1},{1,2},{2,3},{3,4},{4,5},{5,6},{6,7},{7,8},{8,9},{9,10},{10,1... | collective-permute-start | bytes 786440 | tf_op jit(solution)/shard_map/ppermute | solution.py:20
  17.1 1.7 copy-start.5
  18.9 1.0 copy-start.2
  54.3 0.9 copy-start.1
  55.2 34.9 %copy-start.4 = (bf16[1,256,256]{2,1,0:T(8,128)(2,1)S(1)}, bf16[1,256,256]{2,1,0:T(8,128)(2,1)}, u32[]{:S(2)}) copy-start(bf16[1,256,256]{2,1,0:T(8,128)(2,1)} %param.9) | copy-start | bytes 393220
  77.9 10.9 %all-to-all-start.3 = ((f32[16,1,1]{2,1,0:T(1,128)}), f32[16,1,1]{2,1,0:T(1,128)S(1)}, u32[]{:S(2)}, u32[]{:S(2)}) async-start(f32[16,1,1]{2,1,0:T(1,128)} %broadcast_in_dim.53), calls=%async_computation.3 | async-start | bytes 16384 | tf_op jit(solution)/shard_map/all_to_all | solution.py:55
  122.8 7.7 %collective-permute-start.3 = (f32[1,256,256]{2,0,1:T(1,128)S(1)}, f32[1,256,256]{2,0,1:T(1,128)S(1)}, u32[]{:S(2)}, u32[]{:S(2)}) collective-permute-start(f32[1,256,256]{2,0,1:T(1,128)S(1)} %broadcast_multiply_fusion.1), channel_id=1, source_target_pairs={{1,0},{2,1},{3,2},{4,3},{5,4},{6,5},{7,6},{8,7},{9,8},{10,9},{11,1... | collective-permute-start | bytes 786440 | tf_op jit(solution)/shard_map/ppermute | solution.py:22
  125.4 6.3 %collective-permute-start.2 = (f32[1,256,256]{2,0,1:T(1,128)S(1)}, f32[1,256,256]{2,0,1:T(1,128)S(1)}, u32[]{:S(2)}, u32[]{:S(2)}) collective-permute-start(f32[1,256,256]{2,0,1:T(1,128)S(1)} %broadcast_multiply_fusion.1), channel_id=1, source_target_pairs={{0,1},{1,2},{2,3},{3,4},{4,5},{5,6},{6,7},{7,8},{8,9},{9,10},{10,1... | collective-permute-start | bytes 786440 | tf_op jit(solution)/shard_map/ppermute | solution.py:20
  130.5 2.9 copy-start.7
  131.7 1.7 copy-start.9
  184.1 10.9 %all-to-all-start.8 = ((f32[16,1,1]{2,1,0:T(1,128)}), f32[16,1,1]{2,1,0:T(1,128)S(1)}, u32[]{:S(2)}, u32[]{:S(2)}) async-start(f32[16,1,1]{2,1,0:T(1,128)} %broadcast_in_dim.57), calls=%async_computation.8 | async-start | bytes 16384 | tf_op jit(solution)/shard_map/all_to_all | solution.py:55
  196.3 10.9 %all-to-all-start.10 = ((f32[16,1,1]{2,1,0:T(1,128)}), f32[16,1,1]{2,1,0:T(1,128)S(1)}, u32[]{:S(2)}, u32[]{:S(2)}) async-start(f32[16,1,1]{2,1,0:T(1,128)} %broadcast_in_dim.59), calls=%async_computation.10 | async-start | bytes 16384 | tf_op jit(solution)/shard_map/all_to_all | solution.py:55
  239.1 7.7 %collective-permute-start.5 = (f32[1,256,256]{2,0,1:T(1,128)S(1)}, f32[1,256,256]{2,0,1:T(1,128)S(1)}, u32[]{:S(2)}, u32[]{:S(2)}) collective-permute-start(f32[1,256,256]{2,0,1:T(1,128)S(1)} %bitcast.65), channel_id=1, source_target_pairs={{1,0},{2,1},{3,2},{4,3},{5,4},{6,5},{7,6},{8,7},{9,8},{10,9},{11,1... | collective-permute-start | bytes 786440 | tf_op jit(solution)/shard_map/ppermute | solution.py:22
  241.7 6.3 %collective-permute-start.4 = (f32[1,256,256]{2,0,1:T(1,128)S(1)}, f32[1,256,256]{2,0,1:T(1,128)S(1)}, u32[]{:S(2)}, u32[]{:S(2)}) collective-permute-start(f32[1,256,256]{2,0,1:T(1,128)S(1)} %bitcast.66), channel_id=1, source_target_pairs={{0,1},{1,2},{2,3},{3,4},{4,5},{5,6},{6,7},{7,8},{8,9},{9,10},{10,1... | collective-permute-start | bytes 786440 | tf_op jit(solution)/shard_map/ppermute | solution.py:20
  247.9 1.7 copy-start.11
  281.4 43.1 %copy-start.6 = (f32[1,256,256]{2,0,1:T(1,128)S(1)}, f32[1,256,256]{2,0,1:T(1,128)}, u32[]{:S(2)}) copy-start(f32[1,256,256]{2,0,1:T(1,128)} %copy-done.5) | copy-start | bytes 786436
  281.4 43.1 %copy-start.8 = (f32[1,256,256]{2,0,1:T(1,128)S(1)}, f32[1,256,256]{2,0,1:T(1,128)}, u32[]{:S(2)}) copy-start(f32[1,256,256]{2,0,1:T(1,128)} %copy-done.7) | copy-start | bytes 786436
  281.4 43.1 %copy-start.10 = (f32[1,256,256]{2,0,1:T(1,128)S(1)}, f32[1,256,256]{2,0,1:T(1,128)}, u32[]{:S(2)}) copy-start(f32[1,256,256]{2,0,1:T(1,128)} %copy-done.9) | copy-start | bytes 786436
  299.7 11.0 %all-to-all-start.15 = ((f32[16,1,1]{2,1,0:T(1,128)}), f32[16,1,1]{2,1,0:T(1,128)S(1)}, u32[]{:S(2)}, u32[]{:S(2)}) async-start(f32[16,1,1]{2,1,0:T(1,128)} %broadcast_in_dim.63), calls=%async_computation.15 | async-start | bytes 16384 | tf_op jit(solution)/shard_map/all_to_all | solution.py:55
  311.9 11.0 %all-to-all-start.17 = ((f32[16,1,1]{2,1,0:T(1,128)}), f32[16,1,1]{2,1,0:T(1,128)S(1)}, u32[]{:S(2)}, u32[]{:S(2)}) async-start(f32[16,1,1]{2,1,0:T(1,128)} %broadcast_in_dim.65), calls=%async_computation.17 | async-start | bytes 16384 | tf_op jit(solution)/shard_map/all_to_all | solution.py:55
  329.3 1.1 copy-start.3
  330.9 4.1 %collective-permute-start.6 = (f32[2,256,256]{1,2,0:T(8,128)S(1)}, f32[2,256,256]{1,2,0:T(8,128)S(1)}, u32[]{:S(2)}, u32[]{:S(2)}) collective-permute-start(f32[2,256,256]{1,2,0:T(8,128)S(1)} %fusion), channel_id=1, source_target_pairs={{0,1},{1,0},{2,3},{3,2},{4,5},{5,4},{6,7},{7,6},{8,9},{9,8},{10,11... | collective-permute-start | bytes 1572872 | tf_op jit(solution)/shard_map/ppermute | solution.py:81
  (1 other events, 0.7 us)
where the time goes:
time: 337 us; the launch traced here: 336 us
  blocking collectives  180 us (53%)
  starting transfers between devices  44.2 us (13%)
  waiting for transfers between devices  38.4 us (11%)
  other arithmetic  36.7 us (11%)
  local copies, waits for them, and re-layouts  14.8 us (4%)
  matrix products  11.7 us (3%)
  between operations  10.2 us (3%)
    all_to_all x10, blocking collectives, sent_to_all(): return lax.all_to_all(copies, axis, split_axis=0, concat_axis=0, tiled=True)  131 us
    all_to_all x3, blocking collectives, summed_on_arrival(): parts = lax.all_to_all(cut_along(x, dim, devices), axis, 0, 0, tiled=True)  49 us
    all_to_all x5, waiting for transfers between devices, sent_to_all(): return lax.all_to_all(copies, axis, split_axis=0, concat_axis=0, tiled=True)  28.8 us
    all_to_all x5, starting transfers between devices, sent_to_all(): return lax.all_to_all(copies, axis, split_axis=0, concat_axis=0, tiled=True)  19.6 us
    ppermute x3, starting transfers between devices, extended(): lax.ppermute(head, axis, [((i + 1) % count, i) for i in range(ends)])  13.9 us
    broadcast_in_dim x15, local copies, waits for them, and re-layouts, sent_to_all(): copies = jnp.broadcast_to(x, (lax.axis_size(axis), *x.shape))  10.8 us
    ppermute x3, starting transfers between devices, extended(): lax.ppermute(tail, axis, [(i, (i + 1) % count) for i in range(ends)])  8.07 us
    reduce_sum x12, other arithmetic, over_copies(): return jnp.sum(everything, axis=0)  7.7 us
  transfers between devices with their start and end apart: 12, of which 11 were waited for; matrix products, arithmetic and copies ran while one was open for 1% of the time, Pallas kernels for 0%

commit v1 on v0

v1 whole, which is shorter than its diff:
```python
import functools

import jax
import jax.numpy as jnp
from jax import lax
from jax.experimental import pallas as pl
from jax.experimental.pallas import tpu as pltpu
from jax.sharding import PartitionSpec as P

F32 = jnp.float32
BF16 = jnp.bfloat16
MESH = pl.DeviceIdType.MESH
TINY = 1e-6
NN = (((1,), (0,)), ((), ()))
NT = (((1,), (1,)), ((), ()))
TN = (((0,), (0,)), ((), ()))


def near_first(count):
    return sorted(range(1, count), key=lambda d: (min(d, count - d), d))


def split(value):
    high = value.astype(BF16)
    low = (value - high.astype(F32)).astype(BF16)
    return high, low


def three_pass(a, b, dims):
    def dot(u, v):
        return lax.dot_general(u, v, dims, preferred_element_type=F32)

    return dot(a[0], b[0]) + (dot(a[0], b[1]) + dot(a[1], b[0]))


def row_of(values):
    rows, columns = values.shape
    folded = values.reshape(rows // 8, 8, columns).sum(axis=0)
    width = min(columns, 128)
    total = folded[:, :width]
    for at in range(width, columns, width):
        total = total + folded[:, at : at + width]
    return jnp.sum(total, axis=0, keepdims=True)


def kernel(
    X,
    Z,
    S,
    states,
    couple,
    labels,
    psi,
    diag,
    left_hbm,
    right_hbm,
    wave,
    rotated,
    left,
    right,
    left_hl,
    right_hl,
    start,
    diags,
    part,
    rs1,
    rs2_out,
    rs2,
    heff,
    corr,
    xnow,
    hnow,
    mixed,
    mixed_in,
    tiles,
    chosen_hl,
    load_sem,
    ex_send,
    ex_recv,
    rs1_send,
    rs1_recv,
    rs2_send,
    rs2_recv,
    ag_send,
    ag_recv,
    side_send,
    side_recv,
    mix_send,
    mix_recv,
    sum_send,
    sum_recv,
):
    N = psi.shape[0]
    Y = S // 2
    w = N // (X * Z)
    ops = lax.axis_index("ops")
    sec = lax.axis_index("sec")
    x, z = ops // Z, ops % Z
    y, core = sec // 2, sec % 2
    partner = y * 2 + (1 - core)
    outer = (sec + 2 * core - 1 + S) % S

    def at_x(d):
        return {"ops": ((x + d) % X) * Z + z, "sec": sec}

    def at_z(d):
        return {"ops": x * Z + (z + d) % Z, "sec": sec}

    sides = ({"ops": ops, "sec": partner}, {"ops": ops, "sec": outer})
    xcore = [({"ops": ((x + d) % X) * Z + z, "sec": y * 2 + c}) for d in range(X) for c in (core, 1 - core)][1:]
    groups = (
        (x * 2 + core, xcore),
        (z, [at_z(d) for d in range(1, Z)]),
        (y, [{"ops": ops, "sec": ((y + d) % Y) * 2 + core} for d in range(1, Y)]),
    )

    barrier = pltpu.get_barrier_semaphore()
    peers = [device for _, members in groups for device in members] + [sides[1]]
    for device in peers:
        pl.semaphore_signal(barrier, inc=1, device_id=device, device_id_type=MESH)

    loads = [
        pltpu.make_async_copy(left_hbm, left, load_sem.at[0]),
        pltpu.make_async_copy(right_hbm, right, load_sem.at[1]),
    ]
    for load in loads:
        load.start()

    size = states[0]
    rows_at = lax.broadcasted_iota(jnp.int32, (N, N), 0)
    cols_at = lax.broadcasted_iota(jnp.int32, (N, N), 1)
    live = ((rows_at < size) & (cols_at < size)).astype(F32)
    start[0] = psi[...].astype(F32) * live
    diags[0] = diag[...].astype(F32)

    pl.semaphore_wait(barrier, len(peers))

    def send(src, dst, send_sem, recv_sem, device):
        copy = pltpu.make_async_remote_copy(
            src_ref=src,
            dst_ref=dst,
            send_sem=send_sem,
            recv_sem=recv_sem,
            device_id=device,
            device_id_type=MESH,
        )
        copy.start()

    def settle(like, sem):
        pltpu.make_async_copy(like, like, sem).wait()

    for j in range(2):
        send(start.at[0], start.at[1 + j], ex_send.at[j], ex_recv.at[j], sides[j])
    for j in range(2):
        send(diags.at[0], diags.at[1 + j], ex_send.at[2 + j], ex_recv.at[2 + j], sides[j])

    for load in loads:
        load.wait()
    for p in range(2):
        left_hl[0, p], left_hl[1, p] = split(left[p])
        right_hl[0, p], right_hl[1, p] = split(right[p])

    picks = []
    for p in range(2):
        source = couple[p]
        row = []
        for target in (sec, partner, outer):
            row.append(jnp.where((source == target) & (source >= 0), 1.0, 0.0).astype(F32))
        picks.append(row)

    def apply(i, v):
        for p in range(2):
            chosen = picks[p][0] * v[0] + picks[p][1] * v[1] + picks[p][2] * v[2]
            chosen_hl[0, p], chosen_hl[1, p] = split(chosen)
        for p in range(2):
            mixed[i, p] = three_pass(
                (left_hl[0, p], left_hl[1, p]), (chosen_hl[0, p], chosen_hl[1, p]), NN
            )
        send(mixed.at[i], mixed_in.at[i], mix_send.at[i], mix_recv.at[i], sides[0])
        total = None
        for p in range(2):
            term = three_pass(split(mixed[i, p]), (right_hl[0, p], right_hl[1, p]), NT)
            total = term if total is None else total + term
        return total

    def slice_of(index):
        return pl.ds(pl.multiple_of(index * w, w), w)

    def scatter_start(i):
        for dz in reversed(near_first(Z)):
            zc = (z + dz) % Z
            for dx in reversed(near_first(X)):
                src = part.at[i, slice_of(((x + dx) % X) * Z + zc)]
                send(src, rs1.at[i, x, zc], rs1_send.at[i], rs1_recv.at[i, zc], at_x(dx))
        for dx in reversed(near_first(X)):
            src = part.at[i, slice_of(((x + dx) % X) * Z + z)]
            send(src, rs1.at[i, x, z], rs1_send.at[i], rs1_recv.at[i, z], at_x(dx))

    def summed_over_x(i, zc):
        settle(rs1.at[i, pl.ds(0, X - 1), 0], rs1_recv.at[i, zc])
        total = part[i, slice_of(x * Z + zc)]
        for dx in range(1, X):
            total = total + rs1[i, (x + dx) % X, zc]
        return total

    def scatter_middle(i):
        for dz in reversed(near_first(Z)):
            zc = (z + dz) % Z
            rs2_out[i, zc] = summed_over_x(i, zc)
            send(rs2_out.at[i, zc], rs2.at[i, z], rs2_send.at[i], rs2_recv.at[i], at_z(dz))
        rs2_out[i, z] = summed_over_x(i, z)

    def scatter_end(i):
        settle(rs2.at[i, pl.ds(0, Z - 1)], rs2_recv.at[i])
        total = rs2_out[i, z]
        for dz in range(1, Z):
            total = total + rs2[i, (z + dz) % Z]
        rows = lax.broadcasted_iota(jnp.int32, (w, N), 0) + ops * w
        cols = lax.broadcasted_iota(jnp.int32, (w, N), 1)
        mask = ((rows < size) & (cols < size)).astype(F32)
        heff[i, 0, slice_of(ops)] = total * mask

    def to_sides(i, index):
        src = heff.at[i, 0, slice_of(index)]
        for j in (1, 0):
            dst = heff.at[i, 1 + j, slice_of(index)]
            send(src, dst, side_send.at[i, j], side_recv.at[i, j], sides[j])

    def gather_start(i):
        src = heff.at[i, 0, slice_of(ops)]
        for dz in reversed(near_first(Z)):
            send(src, src, ag_send.at[i, 0], ag_recv.at[i, ops], at_z(dz))
        for dx in reversed(near_first(X)):
            send(src, src, ag_send.at[i, 1], ag_recv.at[i, ops], at_x(dx))
        to_sides(i, ops)

    def gather_along_x(i):
        for dz in near_first(Z):
            index = x * Z + (z + dz) % Z
            src = heff.at[i, 0, slice_of(index)]
            settle(src, ag_recv.at[i, index])
            for dx in reversed(near_first(X)):
                send(src, src, ag_send.at[i, 1], ag_recv.at[i, index], at_x(dx))
            to_sides(i, index)

    def gather_end(i):
        for dz in [0] + near_first(Z):
            for dx in near_first(X):
                index = ((x + dx) % X) * Z + (z + dz) % Z
                settle(heff.at[i, 0, slice_of(index)], ag_recv.at[i, index])
                to_sides(i, index)
        for j in range(2):
            settle(heff.at[i, 1 + j], side_recv.at[i, j])

    def reduction_sends_done(i):
        for _ in range(X - 1):
            settle(rs1.at[i, 0], rs1_send.at[i])
            settle(rs1.at[i, 0], ag_send.at[i, 1])
        settle(rs2.at[i, pl.ds(0, Z - 1)], rs2_send.at[i])
        settle(rs2.at[i, pl.ds(0, Z - 1)], ag_send.at[i, 0])
        for j in range(2):
            settle(heff.at[i, 0], side_send.at[i, j])

    def sum_start(i, stage, tile):
        mine, members = groups[stage]
        slot = tiles.at[i, stage, mine]
        slot[...] = tile
        for device in members:
            send(slot, slot, sum_send.at[i, stage], sum_recv.at[i, stage], device)

    def sum_end(i, stage):
        others = len(groups[stage][1])
        settle(tiles.at[i, stage, pl.ds(0, others)], sum_recv.at[i, stage])
        total = tiles[i, stage, 0]
        for slot in range(1, others + 1):
            total = total + tiles[i, stage, slot]
        return total

    def sums_done(i):
        for stage in range(3):
            others = len(groups[stage][1])
            settle(tiles.at[i, stage, pl.ds(0, others)], sum_send.at[i, stage])

    def tile_of(values):
        rows = [row_of(value) for value in values]
        blank = jnp.zeros_like(rows[0])
        tile = jnp.concatenate(rows + [blank] * (8 - len(rows)), axis=0)
        if tile.shape[1] < 128:
            tile = jnp.concatenate([tile, jnp.zeros((8, 128 - tile.shape[1]), F32)], axis=1)
        return tile

    def scalars_of(tile, count):
        columns = jnp.sum(tile, axis=1, keepdims=True)
        return [columns[q : q + 1] for q in range(count)]

    share = 1.0 / (X * Z)

    for j in range(2):
        settle(start.at[1 + j], ex_recv.at[j])
    term = apply(0, start)
    part[0] = term
    scatter_start(0)
    own = start[0]
    sum_start(0, 0, tile_of([own * own * share, own * term]))
    scatter_middle(0)
    sum_start(0, 1, sum_end(0, 0))
    scatter_end(0)
    gather_start(0)
    sum_start(0, 2, sum_end(0, 1))
    gather_along_x(0)
    gather_end(0)
    squares, energy = scalars_of(sum_end(0, 2), 2)
    for j in range(2):
        settle(diags.at[1 + j], ex_recv.at[2 + j])

    factor = lax.rsqrt(squares + TINY)
    theta = energy * factor * factor

    for b in range(3):
        top = factor * heff[0, b] - theta * (factor * start[b])
        corr[0, b] = top / (jnp.abs(diags[b] - theta) + 1.0)

    def turn(tile, theta):
        xt, ct, k, cc, chx, xx, xhx = scalars_of(tile, 7)
        square = jnp.maximum(cc - 2.0 * k * k + k * k * xx, 0.0)
        n = lax.rsqrt(square + TINY)
        middle = 0.5 * n * ((xt - k * xhx) + (chx - k * xhx))
        last = n * n * (ct - k * xt - k * chx + k * k * xhx)
        u, v = last - theta, -2.0 * middle
        most = jnp.maximum(jnp.abs(u), jnp.abs(v))
        safe = jnp.where(most > 0.0, most, 1.0)
        us, vs = u / safe, v / safe
        r = jnp.sqrt(us * us + vs * vs)
        rs = jnp.where(most > 0.0, r, 1.0)
        big = jnp.sqrt(0.5 * (rs + jnp.abs(us)) / rs)
        small = 0.5 * jnp.abs(vs) / (rs * big)
        sign = jnp.where(middle >= 0.0, -1.0, 1.0)
        cosine = jnp.where(u >= 0.0, big, small)
        sine = sign * jnp.where(u >= 0.0, small, big)
        cosine = jnp.where(most > 0.0, cosine, 1.0)
        sine = jnp.where(most > 0.0, sine, 0.0)
        lowest = 0.5 * (theta + last) - 0.5 * jnp.where(most > 0.0, safe * r, 0.0)
        return cosine - sine * n * k, sine * n, lowest

    term = apply(1, corr.at[0])
    part[1] = term
    scatter_start(1)
    own, hown, c = factor * start[0], factor * heff[0, 0], corr[0, 0]
    sum_start(
        1,
        0,
        tile_of(
            [
                own * term,
                c * term,
                own * c * share,
                c * c * share,
                c * hown * share,
                own * own * share,
                own * hown * share,
            ]
        ),
    )
    scatter_middle(1)
    sum_start(1, 1, sum_end(1, 0))
    scatter_end(1)
    gather_start(1)
    sum_start(1, 2, sum_end(1, 1))
    gather_along_x(1)
    gather_end(1)
    alpha, beta, theta = turn(sum_end(1, 2), theta)
    alpha = alpha * factor
    hown = None
    for b in range(3):
        xb = alpha * start[b] + beta * corr[0, b]
        hb = alpha * heff[0, b] + beta * heff[1, b]
        xnow[b] = xb
        corr[1, b] = (hb - theta * xb) / (jnp.abs(diags[b] - theta) + 1.0)
        if hown is None:
            hown = hb
    hnow[...] = hown

    term = apply(2, corr.at[1])
    own, hown, c = xnow[0], hnow[...], corr[1, 0]
    sum_start(
        2,
        0,
        tile_of(
            [
                own * term,
                c * term,
                own * c * share,
                c * c * share,
                c * hown * share,
                own * own * share,
                own * hown * share,
            ]
        ),
    )
    keep = jnp.where(labels[0] == sec, 1.0, 0.0).astype(F32)
    swap = 1.0 - keep
    for i in range(3):
        settle(mixed_in.at[i], mix_recv.at[i])
        settle(mixed_in.at[i], mix_send.at[i])
    for p in range(2):
        first = alpha * mixed[0, p] + beta * mixed[1, p]
        other = alpha * mixed_in[0, p] + beta * mixed_in[1, p]
        left[p] = keep * first + swap * other
        right[p] = keep * mixed[2, p] + swap * mixed_in[2, p]
    sum_start(2, 1, sum_end(2, 0))
    sum_start(2, 2, sum_end(2, 1))
    for i in range(2):
        reduction_sends_done(i)
    for j in range(2):
        settle(start.at[0], ex_send.at[j])
        settle(diags.at[0], ex_send.at[2 + j])
    for i in range(2):
        sums_done(i)
    alpha, beta, theta = turn(sum_end(2, 2), theta)
    scale = jnp.sqrt(jnp.float32(S * N * N))
    alpha, beta = alpha * scale, beta * scale
    wave_own = alpha * xnow[0] + beta * corr[1, 0]
    wave[...] = wave_own
    basis = keep * wave_own + swap * (alpha * xnow[1] + beta * corr[1, 1])
    basis = split(basis * (1.0 / jnp.sqrt(jnp.float32(N))))
    for p in range(2):
        inner = split(alpha * left[p] + beta * right[p])
        rotated[p] = three_pass(basis, inner, TN)
    sums_done(2)


def local(X, sector_states, psi_guess, precond_diag, left_ops, right_ops, couple, new_sector):
    N = psi_guess.shape[1]
    S = lax.axis_size("sec")
    Z = lax.axis_size("ops") // X
    pairs = left_ops.shape[0]
    w = N // (X * Z)
    G = max(2 * X, Z, S // 2)
    dma = pltpu.SemaphoreType.DMA
    smem = pl.BlockSpec(memory_space=pltpu.SMEM)
    vmem = pl.BlockSpec(memory_space=pltpu.VMEM)
    hbm = pl.BlockSpec(memory_space=pl.ANY)
    wave, rotated = pl.pallas_call(
        functools.partial(kernel, X, Z, S),
        out_shape=(
            jax.ShapeDtypeStruct((N, N), F32),
            jax.ShapeDtypeStruct((pairs, N, N), F32),
        ),
        in_specs=[smem, smem, smem, vmem, vmem, hbm, hbm],
        out_specs=(vmem, vmem),
        scratch_shapes=[
            pltpu.VMEM((2, N, N), F32),
            pltpu.VMEM((2, N, N), F32),
            pltpu.VMEM((2, 2, N, N), BF16),
            pltpu.VMEM((2, 2, N, N), BF16),
            pltpu.VMEM((3, N, N), F32),
            pltpu.VMEM((3, N, N), F32),
            pltpu.VMEM((2, N, N), F32),
            pltpu.VMEM((2, X, Z, w, N), F32),
            pltpu.VMEM((2, Z, w, N), F32),
            pltpu.VMEM((2, Z, w, N), F32),
            pltpu.VMEM((2, 3, N, N), F32),
            pltpu.VMEM((2, 3, N, N), F32),
            pltpu.VMEM((3, N, N), F32),
            pltpu.VMEM((N, N), F32),
            pltpu.VMEM((3, 2, N, N), F32),
            pltpu.VMEM((3, 2, N, N), F32),
            pltpu.VMEM((3, 3, G, 8, 128), F32),
            pltpu.VMEM((2, 2, N, N), BF16),
            dma((2,)),
            dma((4,)),
            dma((4,)),
            dma((2,)),
            dma((2, Z)),
            dma((2,)),
            dma((2,)),
            dma((2, 2)),
            dma((2, X * Z)),
            dma((2, 2)),
            dma((2, 2)),
            dma((3,)),
            dma((3,)),
            dma((3, 3)),
            dma((3, 3)),
        ],
        compiler_params=pltpu.CompilerParams(collective_id=0, has_side_effects=True),
    )(
        sector_states,
        couple[:, 0],
        new_sector,
        psi_guess[0],
        precond_diag[0],
        left_ops[:, 0],
        right_ops[:, 0],
    )
    return wave[None], rotated[:, None]


def solution(mesh):
    count = mesh.shape["ops"]
    X = 4 if count == 32 else 2
    in_specs = (
        P("sec"),
        P("sec", None, None),
        P("sec", None, None),
        P("ops", "sec", None, None),
        P("ops", "sec", None, None),
        P("ops", "sec"),
        P("sec"),
    )
    out_specs = (P("sec", None, None), P("ops", "sec", None, None))
    return jax.shard_map(
        functools.partial(local, X), mesh=mesh, in_specs=in_specs, out_specs=out_specs, check_vma=False
    )
```

time: 337 us -> 81.8 us (0.24)
  blocking collectives: 180 us -> 0 us
  Pallas kernels: 0 us -> 77.2 us
  starting transfers between devices: 44.2 us -> 0 us
  waiting for transfers between devices: 38.4 us -> 0 us
  other arithmetic: 36.7 us -> 0 us
  local copies, waits for them, and re-layouts: 14.8 us -> 2.52 us
  matrix products: 11.7 us -> 0 us
  between operations: 10.2 us -> 1.94 us
    all_to_all x13 -> x0, blocking collectives: 180 us -> none  [the longest x10 131 us: sent_to_all(): return lax.all_to_all(copies, axis, split_axis=0, concat_axis=0, tiled=True)]
    pallas_call x0 -> x1, Pallas kernels: none -> 77.2 us  [local(): pl.pallas_call(functools.partial(kernel, X, Z, S), out_shape=(jax.ShapeDt...]
    all_to_all x5 -> x0, waiting for transfers between devices: 28.8 us -> none  [sent_to_all(): return lax.all_to_all(copies, axis, split_axis=0, concat_axis=0, tiled=True)]
    reduce_sum x22 -> x0, other arithmetic: 28.2 us -> none  [the longest x12 7.7 us: over_copies(): return jnp.sum(everything, axis=0)]
    ppermute x7 -> x0, starting transfers between devices: 24.6 us -> none  [the longest x3 13.9 us: extended(): lax.ppermute(head, axis, [((i + 1) % count, i) for i in range(ends)])]
    all_to_all x5 -> x0, starting transfers between devices: 19.6 us -> none  [sent_to_all(): return lax.all_to_all(copies, axis, split_axis=0, concat_axis=0, tiled=True)]
    dot_general x12 -> x0, matrix products: 11.7 us -> none  [the longest x3 5.15 us: product(): chosen = jnp.einsum('pk,kij->pij', picks, wide, precision=HIGH)]
    broadcast_in_dim x15 -> x0, local copies, waits for them, and re-layouts: 10.8 us -> none  [sent_to_all(): copies = jnp.broadcast_to(x, (lax.axis_size(axis), *x.shape))]
  transfers between devices with their start and end apart: 12 -> 0, of which waited for: 11 -> 0; matrix products, arithmetic and copies ran while one was open for 1% -> 0% of each run, Pallas kernels for 0% -> 0%
where the time goes in v1:
time: 81.8 us; the launch traced here: 81.6 us
  Pallas kernels  77.2 us (94%)
  local copies, waits for them, and re-layouts  2.52 us (3%)
  between operations  1.94 us (2%)
    pallas_call x1, Pallas kernels, local(): pl.pallas_call(functools.partial(kernel, X, Z, S), out_shape=(jax.ShapeDt...  77.2 us
    unnamed x4, local copies, waits for them, and re-layouts  2.52 us

profile of v1, /device:TPU:1, one launch (start us, length us, event | category | flops | bytes accessed | tf_op | source)
XLA Modules:
  0.0 81.6 jit_solution(7930991228189878380)
XLA Ops:
  1.9 77.2 %shard_map.86 = (f32[256,256]{1,0:T(8,128)}, f32[2,256,256]{2,1,0:T(8,128)}) custom-call(s32[1]{0:T(128)S(6)} %copy.12.states, s32[2]{0:T(128)} %bitcast.15, s32[1]{0:T(128)S(6)} %copy.13.labels, bf16[256,256]{1,0:T(8,128)(2,1)} %bitcast.13, bf16[256,256]{1,0:T(8,128)(2,1)} %bitcast.14, f32[2,256,256]{2,1,0:T(8,128)} %bitcast.9, f32[2,256,256]{2,1,0:T(8,128)} %bitcast.10), custom_call_target="tpu_custom_call" | custom-call | tf_op jit(solution)/shard_map/pallas_call | solution.py:443
  79.1 0.0 copy-start
  79.1 1.7 %copy.14 = f32[1,256,256]{2,1,0:T(8,128)} copy(f32[1,256,256]{2,1,0:T(8,128)} %bitcast.12) | data formatting | bytes 524288
  80.8 0.0 copy-done
  80.8 0.8 copy.15
Async XLA Ops:
  79.1 1.7 %copy-start = (f32[2,256,256]{2,1,0:T(8,128)S(1)}, f32[2,256,256]{2,1,0:T(8,128)}, u32[]{:S(2)}) copy-start(f32[2,256,256]{2,1,0:T(8,128)} %get-tuple-element.5) | copy-start | bytes 1572868

commit v2 on v1

v2 whole, which is shorter than its diff:
```python
import functools

import jax
import jax.numpy as jnp
from jax import lax
from jax.experimental import pallas as pl
from jax.experimental.pallas import tpu as pltpu
from jax.sharding import PartitionSpec as P

F32 = jnp.float32
BF16 = jnp.bfloat16
MESH = pl.DeviceIdType.MESH
TINY = 1e-6
FAR = 9
BULK = True
HAND_ON = True
NN = (((1,), (0,)), ((), ()))
TN = (((0,), (0,)), ((), ()))


def near_first(count):
    return sorted(range(1, count), key=lambda d: (min(d, count - d), d))


def split(value):
    high = value.astype(BF16)
    low = (value - high.astype(F32)).astype(BF16)
    return high, low


def dot(a, b, dims=NN):
    return lax.dot_general(a, b, dims, preferred_element_type=F32)


def row_of(values):
    rows, columns = values.shape
    folded = values.reshape(rows // 8, 8, columns).sum(axis=0)
    width = min(columns, 128)
    total = folded[:, :width]
    for at in range(width, columns, width):
        total = total + folded[:, at : at + width]
    return jnp.sum(total, axis=0, keepdims=True)


def tile_of(values):
    rows = [row_of(value) for value in values]
    blank = jnp.zeros_like(rows[0])
    tile = jnp.concatenate(rows + [blank] * (8 - len(rows)), axis=0)
    if tile.shape[1] < 128:
        tile = jnp.concatenate([tile, jnp.zeros((8, 128 - tile.shape[1]), F32)], axis=1)
    return tile


def scalars_of(tile, count):
    columns = jnp.sum(tile, axis=1, keepdims=True)
    return [columns[q : q + 1] for q in range(count)]


def turn(tile, theta):
    xt, ct, k, cc, chx, xx, xhx = scalars_of(tile, 7)
    square = jnp.maximum(cc - 2.0 * k * k + k * k * xx, 0.0)
    n = lax.rsqrt(square + TINY)
    middle = 0.5 * n * ((xt - k * xhx) + (chx - k * xhx))
    last = n * n * (ct - k * xt - k * chx + k * k * xhx)
    u, v = last - theta, -2.0 * middle
    most = jnp.maximum(jnp.abs(u), jnp.abs(v))
    safe = jnp.where(most > 0.0, most, 1.0)
    us, vs = u / safe, v / safe
    r = jnp.sqrt(us * us + vs * vs)
    rs = jnp.where(most > 0.0, r, 1.0)
    big = jnp.sqrt(0.5 * (rs + jnp.abs(us)) / rs)
    small = 0.5 * jnp.abs(vs) / (rs * big)
    sign = jnp.where(middle >= 0.0, -1.0, 1.0)
    cosine = jnp.where(u >= 0.0, big, small)
    sine = sign * jnp.where(u >= 0.0, small, big)
    cosine = jnp.where(most > 0.0, cosine, 1.0)
    sine = jnp.where(most > 0.0, sine, 0.0)
    lowest = 0.5 * (theta + last) - 0.5 * jnp.where(most > 0.0, safe * r, 0.0)
    return cosine - sine * n * k, sine * n, lowest


SCRATCH = (
    "left",
    "right",
    "left_cat",
    "right_cat",
    "chosen_cat",
    "mixed_cat",
    "start",
    "diags",
    "gain",
    "shift",
    "partial",
    "part",
    "rs_x",
    "rs_far",
    "rs_out",
    "rs_z",
    "heff",
    "corr",
    "xnow",
    "hnow",
    "mixed",
    "mixed_in",
    "tiles",
    "load_sem",
    "ex_send",
    "ex_recv",
    "rsx_send",
    "rsx_recv",
    "rsf_send",
    "rsf_recv",
    "rsz_send",
    "rsz_recv",
    "agz_send",
    "agx_send",
    "agf_send",
    "ag_recv",
    "side_send",
    "side_recv",
    "mix_send",
    "mix_recv",
    "sum_send",
    "sum_recv",
    "wide_tiles",
    "wide_send",
    "wide_recv",
    "local_tile",
    "turn_cat",
    "quad",
)


def kernel(X, Z, S, states, couple, labels, psi, diag, left_hbm, right_hbm, wave, rotated, *scratch):
    refs = dict(zip(SCRATCH, scratch, strict=True))
    left, right, left_cat, right_cat = (refs[k] for k in SCRATCH[:4])
    chosen_cat, mixed_cat, start, diags, gain, shift, partial, part = (refs[k] for k in SCRATCH[4:12])
    rs_x, rs_far, rs_out, rs_z, heff, corr, xnow, hnow, mixed, mixed_in, tiles = (refs[k] for k in SCRATCH[12:23])
    load_sem, ex_send, ex_recv, rsx_send, rsx_recv, rsf_send, rsf_recv = (refs[k] for k in SCRATCH[23:30])
    rsz_send, rsz_recv, agz_send, agx_send, agf_send, ag_recv, side_send = (refs[k] for k in SCRATCH[30:37])
    side_recv, mix_send, mix_recv, sum_send, sum_recv, wide_tiles, wide_send, wide_recv = (
        refs[k] for k in SCRATCH[37:45]
    )
    local_tile, turn_cat, quad = (refs[k] for k in SCRATCH[45:])
    N = psi.shape[0]
    Y = S // 2
    w = N // (X * Z)
    block = N // X
    ops = lax.axis_index("ops")
    sec = lax.axis_index("sec")
    x, z = ops // Z, ops % Z
    y, core = sec // 2, sec % 2
    partner = y * 2 + (1 - core)
    outer = (sec + 2 * core - 1 + S) % S
    far = [d for d in reversed(near_first(Z)) if min(d, Z - d) >= FAR]
    near = [d for d in near_first(Z) if d not in far]
    around = near_first(X)

    def at(xd, zd):
        return {"ops": xd * Z + zd, "sec": sec}

    def off(dx, dz):
        return at((x + dx) % X, (z + dz) % Z)

    sides = ({"ops": ops, "sec": partner}, {"ops": ops, "sec": outer})
    xcore = [{"ops": ((x + d) % X) * Z + z, "sec": y * 2 + c} for d in range(X) for c in (core, 1 - core)][1:]
    groups = (
        (x * 2 + core, xcore),
        (z, [off(0, d) for d in range(1, Z)]),
        (y, [{"ops": ops, "sec": ((y + d) % Y) * 2 + core} for d in range(1, Y)]),
    )

    plane = [(dx, dz) for dz in reversed([0] + near_first(Z)) for dx in reversed([0] + around) if dx or dz]
    wide_groups = (
        (ops, [off(dx, dz) for dx, dz in plane]),
        (
            sec,
            [
                {"ops": ops, "sec": ((y + d) % Y) * 2 + c}
                for d in reversed([0] + near_first(Y))
                for c in ((1 - core, core) if d else (1 - core,))
            ],
        ),
    )

    barrier = pltpu.get_barrier_semaphore()
    peers = [device for _, members in groups for device in members] + [sides[1]]
    peers += [off(dx, dz) for dx in around for dz in far]
    for device in peers:
        pl.semaphore_signal(barrier, inc=1, device_id=device, device_id_type=MESH)

    loads = [
        pltpu.make_async_copy(left_hbm, left, load_sem.at[0]),
        pltpu.make_async_copy(right_hbm, right, load_sem.at[1]),
    ]
    for load in loads:
        load.start()

    size = states[0]
    rows_at = lax.broadcasted_iota(jnp.int32, (N, N), 0)
    cols_at = lax.broadcasted_iota(jnp.int32, (N, N), 1)
    live = ((rows_at < size) & (cols_at < size)).astype(F32)
    start[0] = psi[...].astype(F32) * live
    diags[0] = diag[...].astype(F32)

    pl.semaphore_wait(barrier, len(peers))

    def send(src, dst, send_sem, recv_sem, device):
        copy = pltpu.make_async_remote_copy(
            src_ref=src,
            dst_ref=dst,
            send_sem=send_sem,
            recv_sem=recv_sem,
            device_id=device,
            device_id_type=MESH,
        )
        copy.start()

    def settle(like, sem):
        pltpu.make_async_copy(like, like, sem).wait()

    for g in range(X):
        rows = pl.ds(g * block, block)
        send(start.at[0, rows], start.at[2, rows], ex_send.at[0], ex_recv.at[g], sides[1])
    send(start.at[0], start.at[1], ex_send.at[1], ex_recv.at[X], sides[0])

    for load in loads:
        load.wait()
    for p in range(2):
        high, low = split(left[p])
        for q, piece in enumerate((high, high, low)):
            left_cat[p, :, q * N : (q + 1) * N] = piece
        high, low = split(right[p].T)
        for q, piece in enumerate((high, low, high)):
            right_cat[(3 * p + q) * N : (3 * p + q + 1) * N] = piece

    picks = []
    for p in range(2):
        source = couple[p]
        row = []
        for target in (sec, partner, outer):
            row.append(jnp.where((source == target) & (source >= 0), 1.0, 0.0).astype(F32))
        picks.append(row)

    def choose_inner(own, other):
        for p in range(2):
            partial[p] = picks[p][0] * own + picks[p][1] * other

    def choose_outer(rows_from, value):
        for p in range(2):
            high, low = split(partial[p, pl.ds(rows_from, block)] + picks[p][2] * value)
            for q, piece in enumerate((high, low, high)):
                chosen_cat[p, pl.ds(q * N + rows_from, block)] = piece

    half = X // 2
    upper = x // half

    def apply_half(i, which):
        rows = pl.ds(pl.multiple_of(which * (N // 2), N // 2), N // 2)
        for p in range(2):
            value = dot(left_cat[p, rows], chosen_cat[p])
            mixed[i, p, rows] = value
            high, low = split(value)
            for q, piece in enumerate((high, high, low)):
                mixed_cat[:, (3 * p + q) * N : (3 * p + q + 1) * N] = piece
        part[i, rows] = dot(mixed_cat[...], right_cat[...])

    def slice_of(index):
        return pl.ds(pl.multiple_of(index * w, w), w)

    def scatter_to(i, xd):
        for f, dz in enumerate(far):
            zd = (z + dz) % Z
            send(part.at[i, slice_of(xd * Z + zd)], rs_far.at[i, x, f], rsf_send.at[i], rsf_recv.at[i], at(xd, zd))

    def scatter_along(i, xd):
        for k, dz in reversed(list(enumerate([0] + near))):
            src = part.at[i, slice_of(xd * Z + (z + dz) % Z)]
            send(src, rs_x.at[i, x, k], rsx_send.at[i], rsx_recv.at[i, k], at(xd, z))

    def apply(i, scatter):
        apply_half(i, 1 - upper)
        away = [(1 - upper) * half + j for j in range(half)]
        beside = [x + 1 - 2 * (x % 2)] if half == 2 else []
        if scatter:
            for xd in away:
                scatter_to(i, xd)
                scatter_along(i, xd)
        apply_half(i, upper)
        if scatter:
            for xd in beside + [x]:
                scatter_to(i, xd)
            for xd in beside:
                scatter_along(i, xd)
        send(mixed.at[i], mixed_in.at[i], mix_send.at[i], mix_recv.at[i], sides[0])

    def summed_over_x(i, k, dz):
        settle(rs_x.at[i, pl.ds(0, X - 1), 0], rsx_recv.at[i, k])
        total = part[i, slice_of(x * Z + (z + dz) % Z)]
        for dx in range(1, X):
            total = total + rs_x[i, (x + dx) % X, k]
        return total

    def scatter_middle(i):
        for k, dz in reversed(list(enumerate([0] + near))):
            rs_out[i, k] = summed_over_x(i, k, dz)
            if k > 0:
                send(rs_out.at[i, k], rs_z.at[i, k], rsz_send.at[i], rsz_recv.at[i], off(0, dz))

    def scatter_end(i):
        total = rs_out[i, 0]
        if near:
            settle(rs_z.at[i, pl.ds(0, len(near))], rsz_recv.at[i])
            for k in range(1, len(near) + 1):
                total = total + rs_z[i, k]
        if far:
            settle(rs_far.at[i], rsf_recv.at[i])
            for xs in range(X):
                for f in range(len(far)):
                    total = total + rs_far[i, xs, f]
        rows = lax.broadcasted_iota(jnp.int32, (w, N), 0) + ops * w
        cols = lax.broadcasted_iota(jnp.int32, (w, N), 1)
        mask = ((rows < size) & (cols < size)).astype(F32)
        heff[i, 0, slice_of(ops)] = total * mask

    def to_sides(i, dx, index):
        src = heff.at[i, 0, slice_of(index)]
        send(src, heff.at[i, 2, slice_of(index)], side_send.at[i, 1], side_recv.at[i, 1 + dx], sides[1])
        if not BULK:
            send(src, heff.at[i, 1, slice_of(index)], side_send.at[i, 0], side_recv.at[i, 0], sides[0])

    def gather_start(i):
        src = heff.at[i, 0, slice_of(ops)]
        for dz in far:
            for dx in list(reversed(around)) + [0]:
                send(src, src, agf_send.at[i], ag_recv.at[i, ops], off(dx, dz))
        for dz in reversed(near):
            send(src, src, agz_send.at[i], ag_recv.at[i, ops], off(0, dz))
        for dx in reversed(around):
            send(src, src, agx_send.at[i], ag_recv.at[i, ops], off(dx, 0))
        to_sides(i, 0, ops)

    def gather_along_x(i):
        for dz in near:
            index = x * Z + (z + dz) % Z
            src = heff.at[i, 0, slice_of(index)]
            settle(src, ag_recv.at[i, index])
            for dx in reversed(around):
                send(src, src, agx_send.at[i], ag_recv.at[i, index], off(dx, 0))
            to_sides(i, 0, index)

    def gather_end(i):
        rest = [(dx, 0) for dx in around] + [(0, dz) for dz in reversed(far)]
        rest += [(dx, dz) for dz in near for dx in around]
        rest += [(dx, dz) for dz in reversed(far) for dx in around]
        for dx, dz in rest:
            index = ((x + dx) % X) * Z + (z + dz) % Z
            settle(heff.at[i, 0, slice_of(index)], ag_recv.at[i, index])
            to_sides(i, dx, index)
        if BULK:
            send(heff.at[i, 0], heff.at[i, 1], side_send.at[i, 0], side_recv.at[i, 0], sides[0])

    def reduction_sends_done(i):
        for _ in range(X - 1):
            settle(rs_x.at[i, 0, pl.ds(0, 1 + len(near))], rsx_send.at[i])
            settle(rs_x.at[i, 0, pl.ds(0, 1 + len(near))], agx_send.at[i])
        if far:
            settle(rs_far.at[i], rsf_send.at[i])
            settle(rs_far.at[i], agf_send.at[i])
        if near:
            settle(rs_z.at[i, pl.ds(0, len(near))], rsz_send.at[i])
            settle(rs_z.at[i, pl.ds(0, len(near))], agz_send.at[i])
        for j in range(2):
            settle(heff.at[i, 0], side_send.at[i, j])

    def sum_start(i, stage, tile):
        mine, members = groups[stage]
        slot = tiles.at[i, stage, mine]
        slot[...] = tile
        for device in members:
            send(slot, slot, sum_send.at[i, stage], sum_recv.at[i, stage], device)

    def sum_end(i, stage):
        others = len(groups[stage][1])
        settle(tiles.at[i, stage, pl.ds(0, others)], sum_recv.at[i, stage])
        total = tiles[i, stage, 0]
        for slot in range(1, others + 1):
            total = total + tiles[i, stage, slot]
        return total

    def sums_done(i):
        for stage in range(3):
            others = len(groups[stage][1])
            settle(tiles.at[i, stage, pl.ds(0, others)], sum_send.at[i, stage])

    def wide_start(stage, row):
        mine, members = wide_groups[stage]
        slot = wide_tiles.at[stage, mine]
        slot[...] = row
        for device in members:
            send(slot, slot, wide_send.at[stage], wide_recv.at[stage], device)

    def wide_end(stage):
        others = len(wide_groups[stage][1])
        settle(wide_tiles.at[stage, pl.ds(0, others)], wide_recv.at[stage])
        totals = [wide_tiles[stage, slot] for slot in range(others + 1)]
        while len(totals) > 1:
            totals = [sum(totals[j : j + 2]) for j in range(0, len(totals), 2)]
        return totals[0]

    def wide_done(stage):
        others = len(wide_groups[stage][1])
        settle(wide_tiles.at[stage, pl.ds(0, others)], wide_send.at[stage])

    lane = lax.broadcasted_iota(jnp.int32, (8, 128), 1)
    sublane = lax.broadcasted_iota(jnp.int32, (8, 128), 0)

    def packed(tile):
        columns = jnp.sum(tile, axis=1, keepdims=True)
        return jnp.sum(jnp.where(lane == sublane, columns, 0.0), axis=0, keepdims=True)

    def unpacked(row):
        return jnp.where(lane == sublane, row, 0.0)

    share = 1.0 / (X * Z)

    def reduce(i, tile):
        sum_start(i, 0, tile)
        scatter_middle(i)
        sum_start(i, 1, sum_end(i, 0))
        scatter_end(i)
        gather_start(i)
        sum_start(i, 2, sum_end(i, 1))
        gather_along_x(i)
        gather_end(i)

    def correct(i, own, hown):
        c = gain[0] * heff[i, 0] - shift[0]
        corr[i, 0] = c
        settle(heff.at[i, 1], side_recv.at[i, 0])
        corr[i, 1] = gain[1] * heff[i, 1] - shift[1]
        choose_inner(corr[i, 0], corr[i, 1])
        rest = [value * share for value in (own * c, c * c, c * hown, own * own, own * hown)]
        local_tile[...] = tile_of([jnp.zeros_like(own)] * 2 + rest)
        for dx in [0] + around:
            rows_from = pl.multiple_of(((x + dx) % X) * block, block)
            rows = pl.ds(rows_from, block)
            settle(heff.at[i, 2, rows], side_recv.at[i, 1 + dx])
            value = gain[2, rows] * heff[i, 2, rows] - shift[2, rows]
            corr[i, 2, rows] = value
            choose_outer(rows_from, value)

    settle(start.at[1], ex_recv.at[X])
    choose_inner(start[0], start[1])
    for g in range(X):
        rows = pl.ds(g * block, block)
        settle(start.at[2, rows], ex_recv.at[g])
        choose_outer(g * block, start[2, rows])
    apply(0, True)
    for j in range(2):
        send(diags.at[0], diags.at[1 + j], ex_send.at[2 + j], ex_recv.at[X + 1 + j], sides[j])
    own, term = start[0], part[0]
    reduce(0, tile_of([own * own * share, own * term]))
    squares, energy = scalars_of(sum_end(0, 2), 2)
    factor = lax.rsqrt(squares + TINY)
    theta = energy * factor * factor
    for j in range(2):
        settle(diags.at[1 + j], ex_recv.at[X + 1 + j])
    for b in range(3):
        inverse = 1.0 / (jnp.abs(diags[b] - theta) + 1.0)
        gain[b] = factor * inverse
        shift[b] = (theta * factor) * start[b] * inverse
    correct(0, factor * start[0], factor * heff[0, 0])

    def products(term, own, c):
        return local_tile[...] + tile_of([own * term, c * term])

    apply(1, True)
    reduce(1, products(part[1], factor * start[0], corr[0, 0]))
    alpha, beta, theta = turn(sum_end(1, 2), theta)
    alpha = alpha * factor
    for b in range(3):
        xb = alpha * start[b] + beta * corr[0, b]
        inverse = 1.0 / (jnp.abs(diags[b] - theta) + 1.0)
        xnow[b] = xb
        gain[b] = beta * inverse
        shift[b] = (theta * xb - alpha * heff[0, b]) * inverse
    hnow[...] = alpha * heff[0, 0] + beta * heff[1, 0]
    correct(1, xnow[0], hnow[...])

    apply(2, False)
    wide_start(0, packed(products(part[2], xnow[0], corr[1, 0])))
    keep = jnp.where(labels[0] == sec, 1.0, 0.0).astype(F32)
    swap = 1.0 - keep
    for i in range(3):
        settle(mixed_in.at[i], mix_recv.at[i])
        settle(mixed_in.at[i], mix_send.at[i])
    root = 1.0 / jnp.sqrt(jnp.float32(N))
    sources = (xnow, corr.at[1])
    for q, source in enumerate(sources):
        value = (keep * source[0] + swap * source[1]) * root
        turn_cat[q, 0], turn_cat[q, 1] = split(value.T)

    def turned_by(q, value):
        high, low = value
        return dot(turn_cat[q, 0], high) + (dot(turn_cat[q, 0], low) + dot(turn_cat[q, 1], high))

    def quadratic(p):
        first = alpha * mixed[0, p] + beta * mixed[1, p]
        other = alpha * mixed_in[0, p] + beta * mixed_in[1, p]
        first = split(keep * first + swap * other)
        second = split(keep * mixed[2, p] + swap * mixed_in[2, p])
        quad[p, 0] = turned_by(0, first)
        quad[p, 1] = turned_by(0, second) + turned_by(1, first)
        quad[p, 2] = turned_by(1, second)

    quadratic(0)
    wide_start(1, wide_end(0))
    quadratic(1)
    for i in range(2):
        reduction_sends_done(i)
        sums_done(i)
    for j in range(2):
        settle(start.at[0], ex_send.at[j])
        settle(diags.at[0], ex_send.at[2 + j])
    wide_done(0)
    alpha, beta, theta = turn(unpacked(wide_end(1)), theta)
    scale = jnp.sqrt(jnp.float32(S * N * N))
    alpha, beta = alpha * scale, beta * scale
    wave[...] = alpha * xnow[0] + beta * corr[1, 0]
    aa, ab, bb = alpha * alpha, alpha * beta, beta * beta
    for p in range(2):
        rotated[p] = (aa * quad[p, 0] + ab * quad[p, 1]) + bb * quad[p, 2]
    wide_done(1)


def handed_on(wave, rotated, wave_out, rotated_out):
    wave_out[...] = wave[...]
    rotated_out[...] = rotated[...]


def local(X, sector_states, psi_guess, precond_diag, left_ops, right_ops, couple, new_sector):
    N = psi_guess.shape[1]
    S = lax.axis_size("sec")
    Z = lax.axis_size("ops") // X
    pairs = left_ops.shape[0]
    w = N // (X * Z)
    G = max(2 * X, Z, S // 2)
    F = max(1, sum(min(d, Z - d) >= FAR for d in range(1, Z)))
    dma = pltpu.SemaphoreType.DMA
    smem = pl.BlockSpec(memory_space=pltpu.SMEM)
    vmem = pl.BlockSpec(memory_space=pltpu.VMEM)
    hbm = pl.BlockSpec(memory_space=pl.ANY)
    shapes = {
        "left": (2, N, N),
        "right": (2, N, N),
        "left_cat": (2, N, 3 * N),
        "right_cat": (6 * N, N),
        "chosen_cat": (2, 3 * N, N),
        "mixed_cat": (N // 2, 6 * N),
        "start": (3, N, N),
        "diags": (3, N, N),
        "gain": (3, N, N),
        "shift": (3, N, N),
        "partial": (2, N, N),
        "part": (3, N, N),
        "rs_x": (2, X, Z, w, N),
        "rs_far": (2, X, F, w, N),
        "rs_out": (2, Z, w, N),
        "rs_z": (2, Z, w, N),
        "heff": (2, 3, N, N),
        "corr": (2, 3, N, N),
        "xnow": (3, N, N),
        "hnow": (N, N),
        "mixed": (3, 2, N, N),
        "mixed_in": (3, 2, N, N),
        "tiles": (2, 3, G, 8, 128),
        "local_tile": (8, 128),
        "turn_cat": (2, 2, N, N),
        "quad": (2, 3, N, N),
        "wide_tiles": (2, max(X * Z, S), 1, 128),
    }
    sems = {
        "load_sem": (2,),
        "ex_send": (4,),
        "ex_recv": (X + 3,),
        "rsx_recv": (2, Z),
        "ag_recv": (2, X * Z),
        "side_send": (2, 2),
        "side_recv": (2, 1 + X),
        "mix_send": (3,),
        "mix_recv": (3,),
        "sum_send": (3, 3),
        "sum_recv": (3, 3),
    }
    scratch = []
    for name in SCRATCH:
        if name in shapes:
            scratch.append(pltpu.VMEM(shapes[name], BF16 if name.endswith("_cat") else F32))
        else:
            scratch.append(dma(sems.get(name, (2,))))
    outs = (
        jax.ShapeDtypeStruct((N, N), F32),
        jax.ShapeDtypeStruct((pairs, N, N), F32),
    )
    wave, rotated = pl.pallas_call(
        functools.partial(kernel, X, Z, S),
        out_shape=(pltpu.VMEM((N, N), F32), pltpu.VMEM((pairs, N, N), F32)),
        in_specs=[smem, smem, smem, vmem, vmem, hbm, hbm],
        out_specs=(vmem, vmem),
        scratch_shapes=scratch,
        compiler_params=pltpu.CompilerParams(collective_id=0, has_side_effects=True),
    )(
        sector_states,
        couple[:, 0],
        new_sector,
        psi_guess[0],
        precond_diag[0],
        left_ops[:, 0],
        right_ops[:, 0],
    )
    if HAND_ON:
        wave, rotated = pl.pallas_call(
            handed_on, out_shape=outs, in_specs=[vmem, vmem], out_specs=(vmem, vmem)
        )(*(pltpu.with_memory_space_constraint(value, pltpu.VMEM) for value in (wave, rotated)))
    return wave[None], rotated[:, None]


def solution(mesh):
    count = mesh.shape["ops"]
    X = 4 if count == 32 else 2
    in_specs = (
        P("sec"),
        P("sec", None, None),
        P("sec", None, None),
        P("ops", "sec", None, None),
        P("ops", "sec", None, None),
        P("ops", "sec"),
        P("sec"),
    )
    out_specs = (P("sec", None, None), P("ops", "sec", None, None))
    return jax.shard_map(
        functools.partial(local, X), mesh=mesh, in_specs=in_specs, out_specs=out_specs, check_vma=False
    )
```

time: 81.8 us -> 75.6 us (0.924)
  Pallas kernels: 77.2 us -> 73.5 us
  local copies, waits for them, and re-layouts: 2.52 us -> 0 us
    pallas_call x1 -> x2, Pallas kernels: 77.2 us -> 73.5 us  [the longest x1 72.6 us: local(): pl.pallas_call(functools.partial(kernel, X, Z, S), out_shape=(pltpu.VMEM(...]
    unnamed x4 -> x0, local copies, waits for them, and re-layouts: 2.52 us -> none
where the time goes in v2:
time: 75.6 us; the launch traced here: 75.4 us
  Pallas kernels  73.5 us (97%)
  between operations  1.93 us (3%)
    pallas_call x1, Pallas kernels, local(): pl.pallas_call(functools.partial(kernel, X, Z, S), out_shape=(pltpu.VMEM(...  72.6 us

profile of v2, /device:TPU:1, one launch (start us, length us, event | category | flops | bytes accessed | tf_op | source)
XLA Modules:
  0.0 75.4 jit_solution(17506557134195606240)
XLA Ops:
  1.9 72.6 %shard_map.86 = (f32[256,256]{1,0:T(8,128)S(1)}, f32[2,256,256]{2,1,0:T(8,128)S(1)}) custom-call(s32[1]{0:T(128)S(6)} %copy.10.states, s32[2]{0:T(128)} %bitcast.13, s32[1]{0:T(128)S(6)} %copy.11.labels, bf16[256,256]{1,0:T(8,128)(2,1)} %bitcast.11, bf16[256,256]{1,0:T(8,128)(2,1)} %bitcast.12, f32[2,256,256]{2,1,0:T(8,128)} %bitcast.9, f32[2,256,256]{2,1,0:T(8,128)} %bitcast.10), custom_call_target="tpu_custom_call" | custom-call | tf_op jit(solution)/shard_map/pallas_call | solution.py:606
  74.5 0.9 %shard_map.87 = (f32[256,256]{1,0:T(8,128)}, f32[2,256,256]{2,1,0:T(8,128)}) custom-call(f32[256,256]{1,0:T(8,128)S(1)} %get-tuple-element.6.wave, f32[2,256,256]{2,1,0:T(8,128)S(1)} %get-tuple-element.7.rotated), custom_call_target="tpu_custom_call" | custom-call | tf_op jit(solution)/shard_map/pallas_call | solution.py:623

commit v3 on v2

--- a/solution.py
+++ b/solution.py
@@ -128,10 +128,12 @@
     "local_tile",
     "turn_cat",
     "quad",
+    "psi",
+    "diag",
 )
 
 
-def kernel(X, Z, S, states, couple, labels, psi, diag, left_hbm, right_hbm, wave, rotated, *scratch):
+def kernel(X, Z, S, states, couple, labels, psi_hbm, diag_hbm, left_hbm, right_hbm, wave, rotated, *scratch):
     refs = dict(zip(SCRATCH, scratch, strict=True))
     left, right, left_cat, right_cat = (refs[k] for k in SCRATCH[:4])
     chosen_cat, mixed_cat, start, diags, gain, shift, partial, part = (refs[k] for k in SCRATCH[4:12])
@@ -141,7 +143,7 @@
     side_recv, mix_send, mix_recv, sum_send, sum_recv, wide_tiles, wide_send, wide_recv = (
         refs[k] for k in SCRATCH[37:45]
     )
-    local_tile, turn_cat, quad = (refs[k] for k in SCRATCH[45:])
+    local_tile, turn_cat, quad, psi, diag = (refs[k] for k in SCRATCH[45:])
     N = psi.shape[0]
     Y = S // 2
     w = N // (X * Z)
@@ -189,17 +191,23 @@
     for device in peers:
         pl.semaphore_signal(barrier, inc=1, device_id=device, device_id_type=MESH)
 
+    early = [
+        pltpu.make_async_copy(psi_hbm, psi, load_sem.at[2]),
+        pltpu.make_async_copy(diag_hbm, diag, load_sem.at[3]),
+    ]
     loads = [
         pltpu.make_async_copy(left_hbm, left, load_sem.at[0]),
         pltpu.make_async_copy(right_hbm, right, load_sem.at[1]),
     ]
-    for load in loads:
+    for load in early + loads:
         load.start()
 
     size = states[0]
     rows_at = lax.broadcasted_iota(jnp.int32, (N, N), 0)
     cols_at = lax.broadcasted_iota(jnp.int32, (N, N), 1)
     live = ((rows_at < size) & (cols_at < size)).astype(F32)
+    for load in early:
+        load.wait()
     start[0] = psi[...].astype(F32) * live
     diags[0] = diag[...].astype(F32)
 
@@ -534,9 +542,15 @@
     wide_done(1)
 
 
-def handed_on(wave, rotated, wave_out, rotated_out):
-    wave_out[...] = wave[...]
-    rotated_out[...] = rotated[...]
+def handed_on(wave, rotated, wave_out, rotated_out, sem):
+    copies = [
+        pltpu.make_async_copy(rotated, rotated_out, sem.at[0]),
+        pltpu.make_async_copy(wave, wave_out, sem.at[1]),
+    ]
+    for copy in copies:
+        copy.start()
+    for copy in copies:
+        copy.wait()
 
 
 def local(X, sector_states, psi_guess, precond_diag, left_ops, right_ops, couple, new_sector):
@@ -578,10 +592,12 @@
         "local_tile": (8, 128),
         "turn_cat": (2, 2, N, N),
         "quad": (2, 3, N, N),
+        "psi": (N, N),
+        "diag": (N, N),
         "wide_tiles": (2, max(X * Z, S), 1, 128),
     }
     sems = {
-        "load_sem": (2,),
+        "load_sem": (4,),
         "ex_send": (4,),
         "ex_recv": (X + 3,),
         "rsx_recv": (2, Z),
@@ -596,7 +612,7 @@
     scratch = []
     for name in SCRATCH:
         if name in shapes:
-            scratch.append(pltpu.VMEM(shapes[name], BF16 if name.endswith("_cat") else F32))
+            scratch.append(pltpu.VMEM(shapes[name], BF16 if name.endswith("_cat") or name in ("psi", "diag") else F32))
         else:
             scratch.append(dma(sems.get(name, (2,))))
     outs = (
@@ -606,7 +622,7 @@
     wave, rotated = pl.pallas_call(
         functools.partial(kernel, X, Z, S),
         out_shape=(pltpu.VMEM((N, N), F32), pltpu.VMEM((pairs, N, N), F32)),
-        in_specs=[smem, smem, smem, vmem, vmem, hbm, hbm],
+        in_specs=[smem, smem, smem, hbm, hbm, hbm, hbm],
         out_specs=(vmem, vmem),
         scratch_shapes=scratch,
         compiler_params=pltpu.CompilerParams(collective_id=0, has_side_effects=True),
@@ -621,7 +637,11 @@
     )
     if HAND_ON:
         wave, rotated = pl.pallas_call(
-            handed_on, out_shape=outs, in_specs=[vmem, vmem], out_specs=(vmem, vmem)
+            handed_on,
+            out_shape=outs,
+            in_specs=[vmem, vmem],
+            out_specs=(hbm, hbm),
+            scratch_shapes=[dma((2,))],
         )(*(pltpu.with_memory_space_constraint(value, pltpu.VMEM) for value in (wave, rotated)))
     return wave[None], rotated[:, None]
 

time: 75.6 us -> 75.2 us (level)
  no operation moved by 1% of the time
where the time goes in v3:
time: 75.2 us; the launch traced here: 75 us
  Pallas kernels  73.1 us (97%)
  between operations  1.93 us (3%)
    pallas_call x1, Pallas kernels, local(): pl.pallas_call(functools.partial(kernel, X, Z, S), out_shape=(pltpu.VMEM(...  72.2 us

profile of v3, /device:TPU:1, one launch (start us, length us, event | category | flops | bytes accessed | tf_op | source)
XLA Modules:
  0.0 75.0 jit_solution(16004233168517505549)
XLA Ops:
  1.9 72.2 %shard_map.86 = (f32[256,256]{1,0:T(8,128)S(1)}, f32[2,256,256]{2,1,0:T(8,128)S(1)}) custom-call(s32[1]{0:T(128)S(6)} %copy.10.states, s32[2]{0:T(128)} %bitcast.13, s32[1]{0:T(128)S(6)} %copy.11.labels, bf16[256,256]{1,0:T(8,128)(2,1)} %bitcast.11, bf16[256,256]{1,0:T(8,128)(2,1)} %bitcast.12, f32[2,256,256]{2,1,0:T(8,128)} %bitcast.9, f32[2,256,256]{2,1,0:T(8,128)} %bitcast.10), custom_call_target="tpu_custom_call" | custom-call | tf_op jit(solution)/shard_map/pallas_call | solution.py:622
  74.1 0.9 %shard_map.87 = (f32[256,256]{1,0:T(8,128)}, f32[2,256,256]{2,1,0:T(8,128)}) custom-call(f32[256,256]{1,0:T(8,128)S(1)} %get-tuple-element.6.wave, f32[2,256,256]{2,1,0:T(8,128)S(1)} %get-tuple-element.7.rotated), custom_call_target="tpu_custom_call" | custom-call | tf_op jit(solution)/shard_map/pallas_call | solution.py:639
